TPU v7x, 128 devices: a whole 4x4x4 slice. The times are simulated.
128 devices in a mesh: member: 16 (over x_lo, y, core), lon: 8 (over x_hi, z).
Axes of the slice: x: 4 (x_hi: 2, x_lo: 2; x = x_hi * 2 + x_lo), y: 4, z: 4, core: 2. Of those that a mesh axis runs over, the one named last changes fastest.
Arguments:
- atmos: bfloat16 [16, 96, 96, 1024], P('member', None, None, 'lon'), may hold values from -6 to 6
- ocean: bfloat16 [96, 96, 1024], P(None, None, 'lon'), may hold values from -6 to 6
- land_mask: int32 [96, 1024], P(None, 'lon'), may hold values 0 or 1
- ice_mask: int32 [96, 1024], P(None, 'lon'), may hold values 0 or 1
- atm_kernel: float32 [2, 7, 7, 96], replicated, may hold values from -0.875 to 0.875
- atm_gain: float32 [2, 96], replicated, may hold values from 0.25 to 1.75
- atm_up: bfloat16 [2, 96, 384], replicated, may hold values from -0.625 to 0.625
- atm_down: bfloat16 [2, 384, 96], replicated, may hold values from -0.3125 to 0.3125
- atm_scale: float32 [2, 96], replicated, may hold values from 0.5 to 1.5
- flux_weight: bfloat16 [96, 32], replicated, may hold values from -0.625 to 0.625
- flux_lift: bfloat16 [2, 32, 96], replicated, may hold values from -1 to 1
- ocn_kernel: float32 [7, 7, 96], replicated, may hold values from -0.875 to 0.875
- ocn_gain: float32 [96], replicated, may hold values from 0.25 to 1.75
- ocn_up: bfloat16 [96, 384], replicated, may hold values from -0.625 to 0.625
- ocn_down: bfloat16 [384, 96], replicated, may hold values from -0.3125 to 0.3125
- ocn_scale: float32 [96], replicated, may hold values from 0.5 to 1.5
- surf_weight: bfloat16 [96, 8], replicated, may hold values from -0.625 to 0.625
- back_weight: bfloat16 [8, 96], replicated, may hold values from -2 to 2
Outputs:
- atmos_out: bfloat16 [16, 96, 96, 1024], P('member', None, None, 'lon')
- ocean_new: bfloat16 [96, 96, 1024], P('member', None, 'lon')
All inputs are finite; a program needn't handle non-finite values. No bound on the sum of `land_mask` or of `ice_mask` on one device may be relied on, other than what follows from the above.
Results may differ from a plain program's by a relative error of at most 0.017.
Values may be sent and summed in bfloat16 or wider, within the bound.
A program may use at most 64 MiB of HBM per device.

v0:
```python
import jax
import jax.numpy as jnp
from jax import lax
from jax.sharding import PartitionSpec as P


def with_halo(cells, sides, width):
    for axis, dim in sides:
        count = lax.axis_size(axis)
        head = lax.slice_in_dim(cells, 0, width, axis=dim)
        tail = lax.slice_in_dim(cells, cells.shape[dim] - width, cells.shape[dim], axis=dim)
        cells = jnp.concatenate(
            [
                lax.ppermute(tail, axis, [(i, (i + 1) % count) for i in range(count)]),
                cells,
                lax.ppermute(head, axis, [((i + 1) % count, i) for i in range(count)]),
            ],
            axis=dim,
        )
    return cells


def contract(form, left, right):
    return jnp.einsum(form, left.astype(jnp.float32), right.astype(jnp.float32))


def mixer(field, padded, kernel, gain, up_proj, down_proj, scale, keep):
    rows = field.shape[0]
    cols = field.shape[2]
    acc = jnp.zeros(field.shape, jnp.float32)
    for i in range(7):
        for j in range(7):
            acc = (
                acc
                + padded[i : i + rows, :, j : j + cols].astype(jnp.float32) * kernel[i, j][:, None]
            )
    center = acc - jnp.mean(acc, axis=1, keepdims=True)
    spread = jnp.mean(center * center, axis=1, keepdims=True)
    normed = (center * lax.rsqrt(spread + 1e-06) * gain[:, None]).astype(jnp.bfloat16)
    hidden = jax.nn.gelu(contract("lcw,ch->lhw", normed, up_proj)).astype(jnp.bfloat16)
    branch = contract("lhw,hc->lcw", hidden, down_proj)
    result = field.astype(jnp.float32) + scale[:, None] * branch
    if keep is not None:
        result = result * keep[:, None, :]
    return result.astype(jnp.bfloat16)


def atmos_pad(state):
    tall = jnp.pad(state, ((3, 3), (0, 0), (0, 0)))
    return with_halo(tall, (("lon", 2),), 3)


def forced(ocean_part, flux_sum, count, sea, ice, flux_lift):
    flux_low = (flux_sum / count).astype(jnp.bfloat16)
    open_term = contract("lfw,fc->lcw", flux_low, flux_lift[0])
    ice_term = contract("lfw,fc->lcw", flux_low, flux_lift[1])
    forcing = sea[:, None, :] * ((1.0 - ice)[:, None, :] * open_term + ice[:, None, :] * ice_term)
    return (ocean_part.astype(jnp.float32) + forcing).astype(jnp.bfloat16)


def local(
    atmos,
    ocean,
    land_mask,
    ice_mask,
    atm_kernel,
    atm_gain,
    atm_up,
    atm_down,
    atm_scale,
    flux_weight,
    flux_lift,
    ocn_kernel,
    ocn_gain,
    ocn_up,
    ocn_down,
    ocn_scale,
    surf_weight,
    back_weight,
):
    sea = (1 - land_mask).astype(jnp.float32)
    ice = ice_mask.astype(jnp.float32)
    state = atmos[0]
    for layer in range(2):
        state = mixer(
            state,
            atmos_pad(state),
            atm_kernel[layer],
            atm_gain[layer],
            atm_up[layer],
            atm_down[layer],
            atm_scale[layer],
            None,
        )
    flux = jax.nn.gelu(contract("lcw,cf->lfw", state, flux_weight))
    members = lax.axis_size("member")
    rank = lax.axis_index("member")
    rows = state.shape[0] // members
    flux_sum = lax.psum(flux.astype(jnp.bfloat16), "member").astype(jnp.float32)
    ocean_mid = forced(ocean, flux_sum, members, sea, ice, flux_lift)
    tall = jnp.pad(ocean_mid, ((3, 3), (0, 0), (0, 0)))
    padded = with_halo(tall, (("lon", 2),), 3)
    ocean_full = mixer(ocean_mid, padded, ocn_kernel, ocn_gain, ocn_up, ocn_down, ocn_scale, sea)
    surface = contract("lcw,cs->lsw", ocean_full, surf_weight).astype(jnp.bfloat16)
    ocean_rows = lax.dynamic_slice_in_dim(ocean_full, rank * rows, rows, 0)
    coupling = sea[:, None, :] * contract("lsw,sc->lcw", surface, back_weight)
    atmos_out = (state.astype(jnp.float32) + coupling).astype(jnp.bfloat16)[None]
    return (atmos_out, ocean_rows)


def solution(mesh):
    in_specs = (
        P("member", None, None, "lon"),
        P(None, None, "lon"),
        P(None, "lon"),
        P(None, "lon"),
        P(),
        P(),
        P(),
        P(),
        P(),
        P(),
        P(),
        P(),
        P(),
        P(),
        P(),
        P(),
        P(),
        P(),
    )
    out_specs = (P("member", None, None, "lon"), P("member", None, "lon"))
    return jax.shard_map(local, mesh=mesh, in_specs=in_specs, out_specs=out_specs, check_vma=False)
```

profile of v0, /device:TPU:1, one launch (start us, length us, event | category | flops | bytes accessed | tf_op | source)
XLA Modules:
  0.0 510.7 jit_solution(5957040996771305564)
XLA Ops:
  7.3 4.7 pad_slice_fusion.245
  11.9 3.3 copy.28
  15.3 2.5 collective-permute-start
  17.8 2.2 copy.31
  20.0 4.8 collective-permute-start.1
  26.9 3.1 copy.29
  30.0 3.0 copy.32
  33.0 83.0 %fusion.313 = (f32[96,128]{1,0:T(8,128)S(1)}, f32[96,96,128]{2,1,0:T(8,128)}) fusion(f32[96]{0:T(128)S(1)} %get-tuple-element.115, bf16[102,96,3]{2,1,0:T(8,128)(2,1)} %copy.32, bf16[102,96,128]{2,1,0:T(8,128)(2,1)S(1)} %pad.10, f32[96]{0:T(128)S(1)} %get-tuple-element.116, f32[96]{0:T(128)S(1)} %get-tuple-element.117, f32[96]{0:T(128)S(1)} %get-tuple-element.118, ...), kind=kLoop, calls=%fused_computation.718 | loop fusion | flops 322031616 | bytes 23932160 | tf_op jit(solution)/shard_map/reduce_sum | solution.py:37
  116.0 3.6 multiply_reduce_fusion.2
  119.6 10.9 %fusion.61 = bf16[96,96,128]{2,1,0:T(8,128)(2,1)} fusion(f32[96]{0:T(128)S(1)} %get-tuple-element.169, f32[96,96,128]{2,1,0:T(8,128)} %get-tuple-element.7, f32[96]{0:T(128)S(1)} %get-tuple-element.164, f32[96,128]{1,0:T(8,128)S(1)} %add_rsqrt_fusion.2, f32[96,128]{1,0:T(8,128)S(1)} %broadcast_multiply_fusion.2, bf16[2,384,96]{1,2,0:T(8,128)(2,1)S(1)} %copy-done.16, ...), kind=kOutput, calls=%fused_computation.304 | convolution fusion | flops 1863843840 | bytes 9683968 | tf_op jit(solution)/shard_map/lhw,hc->lcw/dot_general | solution.py:24
  130.5 4.6 pad_slice_fusion.243
  135.2 3.3 copy.34
  138.6 2.2 copy.37
  140.8 5.1 %collective-permute-start.3 = (bf16[102,96,3]{0,1,2:T(8,128)(2,1)S(1)}, bf16[102,96,3]{0,1,2:T(8,128)(2,1)S(1)}, u32[]{:S(2)}, u32[]{:S(2)}) collective-permute-start(bf16[102,96,3]{0,1,2:T(8,128)(2,1)S(1)} %copy.37), channel_id=1, source_target_pairs={{1,0},{2,1},{3,2},{4,3},{5,4},{6,5},{7,6},{0,7},{9,8},{10,9},{11,1... | collective-permute-start | bytes 176264 | tf_op jit(solution)/shard_map/ppermute | solution.py:16
  147.8 3.5 copy.35
  151.3 3.0 copy.38
  154.3 82.9 %fusion.311 = (f32[96,128]{1,0:T(8,128)S(1)}, f32[96,96,128]{2,1,0:T(8,128)}) fusion(f32[96]{0:T(128)S(1)} %get-tuple-element.66, bf16[102,96,3]{2,1,0:T(8,128)(2,1)} %copy.38, bf16[102,96,128]{2,1,0:T(8,128)(2,1)S(1)} %pad.11, f32[96]{0:T(128)S(1)} %get-tuple-element.67, f32[96]{0:T(128)S(1)} %get-tuple-element.68, f32[96]{0:T(128)S(1)} %get-tuple-element.69, ...), kind=kLoop, calls=%fused_computation.717 | loop fusion | flops 322031616 | bytes 23932160 | tf_op jit(solution)/shard_map/reduce_sum | solution.py:37
  237.3 3.6 multiply_reduce_fusion.1
  240.9 10.9 %fusion.87 = bf16[96,96,128]{2,1,0:T(8,128)(2,1)} fusion(bf16[96,96,128]{2,1,0:T(8,128)(2,1)S(1)} %copy-done.4, f32[96]{0:T(128)S(1)} %get-tuple-element.170, f32[96,96,128]{2,1,0:T(8,128)} %get-tuple-element.5, f32[96]{0:T(128)S(1)} %get-tuple-element.163, f32[96,128]{1,0:T(8,128)S(1)} %add_rsqrt_fusion.1, f32[96,128]{1,0:T(8,128)S(1)} %broadcast_multiply_fusion.1, ...), kind=kOutput, calls=%fused_computation.330 | convolution fusion | flops 1863843840 | bytes 9683968 | tf_op jit(solution)/shard_map/lhw,hc->lcw/dot_general | solution.py:24
  251.8 3.4 fusion.267
  255.3 117.9 %all-reduce.5.cloned.1.call-done = bf16[96,32,128]{2,1,0:T(8,128)(2,1)} async-done(((bf16[96,32,128]{2,1,0:T(8,128)(2,1)}), bf16[96,32,128]{2,1,0:T(8,128)(2,1)}) %all-reduce.5.cloned.1.call-update) | async-done | bytes 786448 | tf_op jit(solution)/shard_map/psum | solution.py:99
  373.2 2.0 fusion.271
  378.3 2.3 pad_slice_fusion.241
  380.6 3.3 copy.40
  385.3 2.2 copy.42
  387.5 3.9 collective-permute-start.5
  393.2 3.3 copy.41
  396.5 3.0 copy.43
  399.6 82.9 %fusion.309 = (f32[96,128]{1,0:T(8,128)S(1)}, f32[96,96,128]{2,1,0:T(8,128)}) fusion(f32[96]{0:T(128)S(1)} %get-tuple-element.63, bf16[102,96,3]{2,1,0:T(8,128)(2,1)} %copy.43, bf16[102,96,128]{2,1,0:T(8,128)(2,1)S(1)} %pad.12, f32[96]{0:T(128)S(1)} %get-tuple-element.64, f32[96]{0:T(128)S(1)} %get-tuple-element.17, f32[96]{0:T(128)S(1)} %get-tuple-element.18, ...), kind=kLoop, calls=%fused_computation.716 | loop fusion | flops 322031616 | bytes 23932160 | tf_op jit(solution)/shard_map/reduce_sum | solution.py:37
  482.5 3.6 multiply_reduce_fusion
  486.2 11.0 %fusion.114 = bf16[96,96,128]{2,1,0:T(8,128)(2,1)} fusion(bf16[96,96,128]{2,1,0:T(8,128)(2,1)S(1)} %copy-done.2, f32[96,128]{1,0:T(8,128)S(1)} %subtract_convert_fusion, f32[96]{0:T(128)S(1)} %copy-done.20, f32[96,96,128]{2,1,0:T(8,128)} %get-tuple-element.3, f32[96]{0:T(128)S(1)} %copy-done.21, f32[96,128]{1,0:T(8,128)S(1)} %add_rsqrt_fusion, ...), kind=kOutput, calls=%fused_computation.357 | convolution fusion | flops 1865023488 | bytes 9732864 | tf_op jit(solution)/shard_map/lhw,hc->lcw/dot_general | solution.py:24
  498.8 4.8 fusion.117
  (80 shorter events, 12.0 us)
Async XLA Ops:
  7.2 478.9 %copy-start = (bf16[384,96]{0,1:T(8,128)(2,1)S(1)}, bf16[384,96]{0,1:T(8,128)(2,1)}, u32[]{:S(2)}) copy-start(bf16[384,96]{0,1:T(8,128)(2,1)} %param.32) | copy-start | bytes 221188
  7.2 366.0 %all-reduce.5.cloned.1.call-start = ((), (), s32[]{:S(2)}) async-start(), calls=%async_computation | async-start | bytes 1572864 | tf_op jit(solution)/shard_map/psum | solution.py:99
  7.2 17.6 %copy-start.8 = (f32[2,7,7,96]{3,0,2,1:T(2,128)S(1)}, f32[2,7,7,96]{3,0,2,1:T(2,128)}, u32[]{:S(2)}) copy-start(f32[2,7,7,96]{3,0,2,1:T(2,128)} %param.22) | copy-start | bytes 112900
  7.2 17.8 %copy-start.14 = (f32[2,96]{1,0:T(2,128)S(1)}, f32[2,96]{1,0:T(2,128)}, u32[]{:S(2)}) copy-start(f32[2,96]{1,0:T(2,128)} %param.23) | copy-start | bytes 2308
  7.2 17.8 %copy-start.15 = (f32[2,96]{1,0:T(2,128)S(1)}, f32[2,96]{1,0:T(2,128)}, u32[]{:S(2)}) copy-start(f32[2,96]{1,0:T(2,128)} %param.26) | copy-start | bytes 2308
  15.3 11.6 %collective-permute-start = (bf16[102,96,3]{0,1,2:T(8,128)(2,1)S(1)}, bf16[102,96,3]{0,1,2:T(8,128)(2,1)S(1)}, u32[]{:S(2)}, u32[]{:S(2)}) collective-permute-start(bf16[102,96,3]{0,1,2:T(8,128)(2,1)S(1)} %copy.28), channel_id=1, source_target_pairs={{0,1},{1,2},{2,3},{3,4},{4,5},{5,6},{6,7},{7,0},{8,9},{9,10},{10,1... | collective-permute-start | bytes 176264 | tf_op jit(solution)/shard_map/ppermute | solution.py:14
  20.0 10.0 %collective-permute-start.1 = (bf16[102,96,3]{0,1,2:T(8,128)(2,1)S(1)}, bf16[102,96,3]{0,1,2:T(8,128)(2,1)S(1)}, u32[]{:S(2)}, u32[]{:S(2)}) collective-permute-start(bf16[102,96,3]{0,1,2:T(8,128)(2,1)S(1)} %copy.31), channel_id=1, source_target_pairs={{1,0},{2,1},{3,2},{4,3},{5,4},{6,5},{7,6},{0,7},{9,8},{10,9},{11,1... | collective-permute-start | bytes 176264 | tf_op jit(solution)/shard_map/ppermute | solution.py:16
  116.0 3.6 copy-start.3
  116.0 3.6 copy-start.16
  116.0 3.6 copy-start.17
  138.5 9.3 %collective-permute-start.2 = (bf16[102,96,3]{0,1,2:T(8,128)(2,1)S(1)}, bf16[102,96,3]{0,1,2:T(8,128)(2,1)S(1)}, u32[]{:S(2)}, u32[]{:S(2)}) collective-permute-start(bf16[102,96,3]{0,1,2:T(8,128)(2,1)S(1)} %copy.34), channel_id=1, source_target_pairs={{0,1},{1,2},{2,3},{3,4},{4,5},{5,6},{6,7},{7,0},{8,9},{9,10},{10,1... | collective-permute-start | bytes 176264 | tf_op jit(solution)/shard_map/ppermute | solution.py:14
  140.8 10.4 %collective-permute-start.3 = (bf16[102,96,3]{0,1,2:T(8,128)(2,1)S(1)}, bf16[102,96,3]{0,1,2:T(8,128)(2,1)S(1)}, u32[]{:S(2)}, u32[]{:S(2)}) collective-permute-start(bf16[102,96,3]{0,1,2:T(8,128)(2,1)S(1)} %copy.37), channel_id=1, source_target_pairs={{1,0},{2,1},{3,2},{4,3},{5,4},{6,5},{7,6},{0,7},{9,8},{10,9},{11,1... | collective-permute-start | bytes 176264 | tf_op jit(solution)/shard_map/ppermute | solution.py:16
  237.2 3.6 copy-start.4
  240.9 10.9 %copy-start.19 = (bf16[96,32]{0,1:T(8,128)(2,1)S(1)}, bf16[96,32]{0,1:T(8,128)(2,1)}, u32[]{:S(2)}) copy-start(bf16[96,32]{0,1:T(8,128)(2,1)} %param.27) | copy-start | bytes 18436
  251.7 3.5 copy-start.10
  251.7 3.5 copy-start.7
  251.7 3.6 copy-start.9
  251.7 121.4 %copy-start.11 = (bf16[2,32,96]{2,1,0:T(8,128)(2,1)S(1)}, bf16[2,32,96]{2,1,0:T(8,128)(2,1)}, u32[]{:S(2)}) copy-start(bf16[2,32,96]{2,1,0:T(8,128)(2,1)} %param.28) | copy-start | bytes 36868
  251.8 123.4 %copy-start.6 = (bf16[96,96,128]{2,1,0:T(8,128)(2,1)S(1)}, bf16[96,96,128]{2,1,0:T(8,128)(2,1)}, u32[]{:S(2)}) copy-start(bf16[96,96,128]{2,1,0:T(8,128)(2,1)} %param.19) | copy-start | bytes 7077892
  373.2 2.0 copy-start.5
  376.9 1.4 copy-start.1
  383.9 9.3 %collective-permute-start.4 = (bf16[102,96,3]{0,1,2:T(8,128)(2,1)S(1)}, bf16[102,96,3]{0,1,2:T(8,128)(2,1)S(1)}, u32[]{:S(2)}, u32[]{:S(2)}) collective-permute-start(bf16[102,96,3]{0,1,2:T(8,128)(2,1)S(1)} %copy.40), channel_id=1, source_target_pairs={{0,1},{1,2},{2,3},{3,4},{4,5},{5,6},{6,7},{7,0},{8,9},{9,10},{10,1... | collective-permute-start | bytes 176264 | tf_op jit(solution)/shard_map/ppermute | solution.py:14
  387.5 9.0 %collective-permute-start.5 = (bf16[102,96,3]{0,1,2:T(8,128)(2,1)S(1)}, bf16[102,96,3]{0,1,2:T(8,128)(2,1)S(1)}, u32[]{:S(2)}, u32[]{:S(2)}) collective-permute-start(bf16[102,96,3]{0,1,2:T(8,128)(2,1)S(1)} %copy.42), channel_id=1, source_target_pairs={{1,0},{2,1},{3,2},{4,3},{5,4},{6,5},{7,6},{0,7},{9,8},{10,9},{11,1... | collective-permute-start | bytes 176264 | tf_op jit(solution)/shard_map/ppermute | solution.py:16
  482.4 3.7 copy-start.2
  482.5 3.7 copy-start.18
  482.5 3.7 copy-start.20
  482.5 3.7 copy-start.21
  486.1 12.6 %copy-start.12 = (bf16[8,96]{1,0:T(8,128)(2,1)S(1)}, bf16[8,96]{1,0:T(8,128)(2,1)}, u32[]{:S(2)}) copy-start(bf16[8,96]{1,0:T(8,128)(2,1)} %param.35) | copy-start | bytes 4612
  486.2 12.6 %copy-start.13 = (bf16[96,8]{0,1:T(8,128)(2,1)S(1)}, bf16[96,8]{0,1:T(8,128)(2,1)}, u32[]{:S(2)}) copy-start(bf16[96,8]{0,1:T(8,128)(2,1)} %param.34) | copy-start | bytes 4612
Sparse Core Ops, SparseCore 0:
  255.3 117.8 all-reduce.4
where the time goes:
time: 514 us; the launch traced here: 511 us
  other arithmetic  260 us (51%)
  waiting for transfers between devices  118 us (23%)
  local copies, waits for them, and re-layouts  55.9 us (11%)
  matrix products  44.7 us (9%)
  starting transfers between devices  17.8 us (3%)
  between operations  14.9 us (3%)
    reduce_sum x3, other arithmetic, mixer(): center = acc - jnp.mean(acc, axis=1, keepdims=True)  249 us
    psum x1, waiting for transfers between devices, local(): flux_sum = lax.psum(flux.astype(jnp.bfloat16), 'member').astype(jnp.float32)  118 us
    dot_general x7, matrix products, contract(): return jnp.einsum(form, left.astype(jnp.float32), right.astype(jnp.float32))  44.7 us
    slice x6, local copies, waits for them, and re-layouts, with_halo(): lax.slice_in_dim(cells, cells.shape[dim] - width, cells.shape[dim], axis=...  21.6 us
    ppermute x3, starting transfers between devices, with_halo(): lax.ppermute(head, axis, [((i + 1) % count, i) for i in range(count)])  13.8 us
    reduce_sum x3, other arithmetic, mixer(): spread = jnp.mean(center * center, axis=1, keepdims=True)  10.7 us
  transfers between devices with their start and end apart: 7, of which 1 were waited for; matrix products, arithmetic and copies ran while one was open for 4% of the time, Pallas kernels for 0%

commit v1 on v0

--- a/solution.py
+++ b/solution.py
@@ -2,6 +2,7 @@
 import jax.numpy as jnp
 from jax import lax
 from jax.sharding import PartitionSpec as P
+from jax.lax import all_gather
 
 
 def with_halo(cells, sides, width):
@@ -96,7 +97,7 @@
     members = lax.axis_size("member")
     rank = lax.axis_index("member")
     rows = state.shape[0] // members
-    flux_sum = lax.psum(flux.astype(jnp.bfloat16), "member").astype(jnp.float32)
+    flux_sum = jnp.sum(all_gather(flux.astype(jnp.bfloat16), "member"), axis=0).astype(jnp.float32)
     ocean_mid = forced(ocean, flux_sum, members, sea, ice, flux_lift)
     tall = jnp.pad(ocean_mid, ((3, 3), (0, 0), (0, 0)))
     padded = with_halo(tall, (("lon", 2),), 3)

time: 514 us -> 477 us (0.928)
  waiting for transfers between devices: 118 us -> 71.7 us
  other arithmetic: 260 us -> 269 us
    psum x1 -> x0, waiting for transfers between devices: 118 us -> none  [local(): flux_sum = lax.psum(flux.astype(jnp.bfloat16), 'member').astype(jnp.float32)]
    all_gather x0 -> x1, waiting for transfers between devices: none -> 71.7 us  [local(): all_gather(flux.astype(jnp.bfloat16), 'member')]
    reduce_sum x0 -> x1, other arithmetic: none -> 6.81 us  [local(): jnp.sum(all_gather(flux.astype(jnp.bfloat16), 'member'), axis=0)]
  transfers between devices with their start and end apart: 7 -> 7, of which waited for: 1 -> 1; matrix products, arithmetic and copies ran while one was open for 4% -> 5% of each run, Pallas kernels for 0% -> 0%
where the time goes in v1:
time: 477 us; the launch traced here: 473 us
  other arithmetic  269 us (56%)
  waiting for transfers between devices  71.7 us (15%)
  local copies, waits for them, and re-layouts  56.5 us (12%)
  matrix products  43.4 us (9%)
  starting transfers between devices  17.9 us (4%)
  between operations  14.8 us (3%)
    reduce_sum x3, other arithmetic, mixer(): center = acc - jnp.mean(acc, axis=1, keepdims=True)  251 us
    all_gather x1, waiting for transfers between devices, local(): all_gather(flux.astype(jnp.bfloat16), 'member')  71.7 us
    dot_general x7, matrix products, contract(): return jnp.einsum(form, left.astype(jnp.float32), right.astype(jnp.float32))  43.4 us
    slice x6, local copies, waits for them, and re-layouts, with_halo(): lax.slice_in_dim(cells, cells.shape[dim] - width, cells.shape[dim], axis=...  21.6 us
    ppermute x3, starting transfers between devices, with_halo(): lax.ppermute(head, axis, [((i + 1) % count, i) for i in range(count)])  13.9 us
    reduce_sum x3, other arithmetic, mixer(): spread = jnp.mean(center * center, axis=1, keepdims=True)  10.7 us
  transfers between devices with their start and end apart: 7, of which 1 were waited for; matrix products, arithmetic and copies ran while one was open for 5% of the time, Pallas kernels for 0%

profile of v1, /device:TPU:1, one launch (start us, length us, event | category | flops | bytes accessed | tf_op | source)
XLA Modules:
  0.0 473.1 jit_solution(7774750909527791697)
XLA Ops:
  7.3 4.7 pad_slice_fusion.245
  11.9 3.3 copy.28
  15.3 2.5 collective-permute-start
  17.8 2.2 copy.31
  20.0 4.8 %collective-permute-start.1 = (bf16[102,96,3]{0,1,2:T(8,128)(2,1)S(1)}, bf16[102,96,3]{0,1,2:T(8,128)(2,1)S(1)}, u32[]{:S(2)}, u32[]{:S(2)}) collective-permute-start(bf16[102,96,3]{0,1,2:T(8,128)(2,1)S(1)} %copy.31), channel_id=1, source_target_pairs={{1,0},{2,1},{3,2},{4,3},{5,4},{6,5},{7,6},{0,7},{9,8},{10,9},{11,1... | collective-permute-start | bytes 176264 | tf_op jit(solution)/shard_map/ppermute | solution.py:17
  26.9 3.0 copy.29
  29.9 3.0 copy.32
  32.9 83.6 %fusion.313 = (f32[96,128]{1,0:T(8,128)S(1)}, f32[96,96,128]{2,1,0:T(8,128)}) fusion(f32[96]{0:T(128)S(1)} %get-tuple-element.115, bf16[102,96,3]{2,1,0:T(8,128)(2,1)} %copy.32, bf16[102,96,128]{2,1,0:T(8,128)(2,1)S(1)} %pad.10, f32[96]{0:T(128)S(1)} %get-tuple-element.116, f32[96]{0:T(128)S(1)} %get-tuple-element.117, f32[96]{0:T(128)S(1)} %get-tuple-element.118, ...), kind=kLoop, calls=%fused_computation.718 | loop fusion | flops 322031616 | bytes 23932160 | tf_op jit(solution)/shard_map/reduce_sum | solution.py:38
  116.6 3.6 multiply_reduce_fusion.2
  120.2 10.9 %fusion.61 = bf16[96,96,128]{2,1,0:T(8,128)(2,1)} fusion(f32[96]{0:T(128)S(1)} %get-tuple-element.169, f32[96,96,128]{2,1,0:T(8,128)} %get-tuple-element.7, f32[96]{0:T(128)S(1)} %get-tuple-element.164, f32[96,128]{1,0:T(8,128)S(1)} %add_rsqrt_fusion.2, f32[96,128]{1,0:T(8,128)S(1)} %broadcast_multiply_fusion.2, bf16[2,384,96]{1,2,0:T(8,128)(2,1)S(1)} %copy-done.15, ...), kind=kOutput, calls=%fused_computation.304 | convolution fusion | flops 1863843840 | bytes 9683968 | tf_op jit(solution)/shard_map/lhw,hc->lcw/dot_general | solution.py:25
  131.1 4.6 pad_slice_fusion.243
  135.8 3.3 copy.34
  139.2 2.2 copy.37
  141.4 5.1 %collective-permute-start.3 = (bf16[102,96,3]{0,1,2:T(8,128)(2,1)S(1)}, bf16[102,96,3]{0,1,2:T(8,128)(2,1)S(1)}, u32[]{:S(2)}, u32[]{:S(2)}) collective-permute-start(bf16[102,96,3]{0,1,2:T(8,128)(2,1)S(1)} %copy.37), channel_id=1, source_target_pairs={{1,0},{2,1},{3,2},{4,3},{5,4},{6,5},{7,6},{0,7},{9,8},{10,9},{11,1... | collective-permute-start | bytes 176264 | tf_op jit(solution)/shard_map/ppermute | solution.py:17
  148.4 3.4 copy.35
  151.8 3.0 copy.38
  154.8 83.7 %fusion.311 = (f32[96,128]{1,0:T(8,128)S(1)}, f32[96,96,128]{2,1,0:T(8,128)}) fusion(f32[96]{0:T(128)S(1)} %get-tuple-element.66, bf16[102,96,3]{2,1,0:T(8,128)(2,1)} %copy.38, bf16[102,96,128]{2,1,0:T(8,128)(2,1)S(1)} %pad.11, f32[96]{0:T(128)S(1)} %get-tuple-element.67, f32[96]{0:T(128)S(1)} %get-tuple-element.68, f32[96]{0:T(128)S(1)} %get-tuple-element.69, ...), kind=kLoop, calls=%fused_computation.717 | loop fusion | flops 322031616 | bytes 23932160 | tf_op jit(solution)/shard_map/reduce_sum | solution.py:38
  238.6 3.6 multiply_reduce_fusion.1
  242.2 10.9 %fusion.87 = bf16[96,96,128]{2,1,0:T(8,128)(2,1)} fusion(bf16[96,96,128]{2,1,0:T(8,128)(2,1)S(1)} %copy-done.4, f32[96]{0:T(128)S(1)} %get-tuple-element.170, f32[96,96,128]{2,1,0:T(8,128)} %get-tuple-element.5, f32[96]{0:T(128)S(1)} %get-tuple-element.163, f32[96,128]{1,0:T(8,128)S(1)} %add_rsqrt_fusion.1, f32[96,128]{1,0:T(8,128)S(1)} %broadcast_multiply_fusion.1, ...), kind=kOutput, calls=%fused_computation.330 | convolution fusion | flops 1863843840 | bytes 9683968 | tf_op jit(solution)/shard_map/lhw,hc->lcw/dot_general | solution.py:25
  253.1 3.3 fusion.267
  256.6 71.7 %all-gather.3.cloned.1.call-done = bf16[1536,32,128]{2,1,0:T(8,128)(2,1)} async-done(((bf16[96,32,128]{2,1,0:T(8,128)(2,1)}), bf16[1536,32,128]{2,1,0:T(8,128)(2,1)}) %all-gather.3.cloned.1.call-update) | async-done | bytes 12582928 | tf_op jit(solution)/shard_map/all_gather | solution.py:100
  328.3 6.8 %reduce_sum.70 = bf16[96,32,128]{2,1,0:T(8,128)(2,1)S(1)} reduce(bf16[16,96,32,128]{3,2,1,0:T(8,128)(2,1)} %bitcast.397, bf16[]{:T(256)} %constant.15.clone.1), dimensions={0}, to_apply=%region_4.5 | reduce | flops 5898240 | bytes 13369346 | tf_op jit(solution)/shard_map/reduce_sum | solution.py:100
  339.8 2.3 pad_slice_fusion.241
  342.1 3.3 copy.40
  346.8 2.4 copy.42
  349.2 3.9 collective-permute-start.5
  355.0 3.0 copy.41
  358.0 3.0 copy.43
  361.0 83.8 %fusion.309 = (f32[96,128]{1,0:T(8,128)S(1)}, f32[96,96,128]{2,1,0:T(8,128)}) fusion(f32[96]{0:T(128)S(1)} %get-tuple-element.63, bf16[102,96,3]{2,1,0:T(8,128)(2,1)} %copy.43, bf16[102,96,128]{2,1,0:T(8,128)(2,1)S(1)} %pad.12, f32[96]{0:T(128)S(1)} %get-tuple-element.64, f32[96]{0:T(128)S(1)} %get-tuple-element.17, f32[96]{0:T(128)S(1)} %get-tuple-element.18, ...), kind=kLoop, calls=%fused_computation.716 | loop fusion | flops 322031616 | bytes 23932160 | tf_op jit(solution)/shard_map/reduce_sum | solution.py:38
  444.9 3.6 multiply_reduce_fusion
  448.5 11.0 %fusion.114 = bf16[96,96,128]{2,1,0:T(8,128)(2,1)} fusion(bf16[96,96,128]{2,1,0:T(8,128)(2,1)S(1)} %copy-done.2, f32[96,128]{1,0:T(8,128)S(1)} %subtract_convert_fusion, f32[96]{0:T(128)S(1)} %copy-done.19, f32[96,96,128]{2,1,0:T(8,128)} %get-tuple-element.3, f32[96]{0:T(128)S(1)} %copy-done.20, f32[96,128]{1,0:T(8,128)S(1)} %add_rsqrt_fusion, ...), kind=kOutput, calls=%fused_computation.357 | convolution fusion | flops 1865023488 | bytes 9732864 | tf_op jit(solution)/shard_map/lhw,hc->lcw/dot_general | solution.py:25
  461.2 4.8 %fusion.117 = bf16[1,96,96,128]{3,2,1,0:T(8,128)(2,1)} fusion(bf16[96,96,128]{2,1,0:T(8,128)(2,1)} %fusion.87, f32[96,128]{1,0:T(8,128)S(1)} %subtract_convert_fusion, bf16[96,96,128]{2,1,0:T(8,128)(2,1)} %fusion.114, bf16[8,96]{1,0:T(8,128)(2,1)S(1)} %copy-done.11, bf16[96,8]{0,1:T(8,128)(2,1)S(1)} %copy-done.12), kind=kOutput, calls=%fused_computation.369 | convolution fusion | flops 42565632 | bytes 7130112 | tf_op jit(solution)/shard_map/lsw,sc->lcw/dot_general | solution.py:25
  (79 shorter events, 13.6 us)
Async XLA Ops:
  7.2 441.3 %copy-start = (bf16[384,96]{0,1:T(8,128)(2,1)S(1)}, bf16[384,96]{0,1:T(8,128)(2,1)}, u32[]{:S(2)}) copy-start(bf16[384,96]{0,1:T(8,128)(2,1)} %param.32) | copy-start | bytes 221188
  7.2 321.1 %all-gather.3.cloned.1.call-start = ((), (), s32[]{:S(2)}) async-start(), calls=%async_computation | async-start | bytes 13369344 | tf_op jit(solution)/shard_map/all_gather | solution.py:100
  7.2 17.6 %copy-start.7 = (f32[2,7,7,96]{3,0,2,1:T(2,128)S(1)}, f32[2,7,7,96]{3,0,2,1:T(2,128)}, u32[]{:S(2)}) copy-start(f32[2,7,7,96]{3,0,2,1:T(2,128)} %param.22) | copy-start | bytes 112900
  7.2 17.8 %copy-start.13 = (f32[2,96]{1,0:T(2,128)S(1)}, f32[2,96]{1,0:T(2,128)}, u32[]{:S(2)}) copy-start(f32[2,96]{1,0:T(2,128)} %param.23) | copy-start | bytes 2308
  7.2 17.8 %copy-start.14 = (f32[2,96]{1,0:T(2,128)S(1)}, f32[2,96]{1,0:T(2,128)}, u32[]{:S(2)}) copy-start(f32[2,96]{1,0:T(2,128)} %param.26) | copy-start | bytes 2308
  15.3 11.6 %collective-permute-start = (bf16[102,96,3]{0,1,2:T(8,128)(2,1)S(1)}, bf16[102,96,3]{0,1,2:T(8,128)(2,1)S(1)}, u32[]{:S(2)}, u32[]{:S(2)}) collective-permute-start(bf16[102,96,3]{0,1,2:T(8,128)(2,1)S(1)} %copy.28), channel_id=1, source_target_pairs={{0,1},{1,2},{2,3},{3,4},{4,5},{5,6},{6,7},{7,0},{8,9},{9,10},{10,1... | collective-permute-start | bytes 176264 | tf_op jit(solution)/shard_map/ppermute | solution.py:15
  20.0 9.9 %collective-permute-start.1 = (bf16[102,96,3]{0,1,2:T(8,128)(2,1)S(1)}, bf16[102,96,3]{0,1,2:T(8,128)(2,1)S(1)}, u32[]{:S(2)}, u32[]{:S(2)}) collective-permute-start(bf16[102,96,3]{0,1,2:T(8,128)(2,1)S(1)} %copy.31), channel_id=1, source_target_pairs={{1,0},{2,1},{3,2},{4,3},{5,4},{6,5},{7,6},{0,7},{9,8},{10,9},{11,1... | collective-permute-start | bytes 176264 | tf_op jit(solution)/shard_map/ppermute | solution.py:17
  116.6 3.6 copy-start.3
  116.6 3.6 copy-start.15
  116.6 3.6 copy-start.16
  139.1 9.3 %collective-permute-start.2 = (bf16[102,96,3]{0,1,2:T(8,128)(2,1)S(1)}, bf16[102,96,3]{0,1,2:T(8,128)(2,1)S(1)}, u32[]{:S(2)}, u32[]{:S(2)}) collective-permute-start(bf16[102,96,3]{0,1,2:T(8,128)(2,1)S(1)} %copy.34), channel_id=1, source_target_pairs={{0,1},{1,2},{2,3},{3,4},{4,5},{5,6},{6,7},{7,0},{8,9},{9,10},{10,1... | collective-permute-start | bytes 176264 | tf_op jit(solution)/shard_map/ppermute | solution.py:15
  141.4 10.4 %collective-permute-start.3 = (bf16[102,96,3]{0,1,2:T(8,128)(2,1)S(1)}, bf16[102,96,3]{0,1,2:T(8,128)(2,1)S(1)}, u32[]{:S(2)}, u32[]{:S(2)}) collective-permute-start(bf16[102,96,3]{0,1,2:T(8,128)(2,1)S(1)} %copy.37), channel_id=1, source_target_pairs={{1,0},{2,1},{3,2},{4,3},{5,4},{6,5},{7,6},{0,7},{9,8},{10,9},{11,1... | collective-permute-start | bytes 176264 | tf_op jit(solution)/shard_map/ppermute | solution.py:17
  238.6 3.6 copy-start.4
  242.2 10.9 %copy-start.18 = (bf16[96,32]{0,1:T(8,128)(2,1)S(1)}, bf16[96,32]{0,1:T(8,128)(2,1)}, u32[]{:S(2)}) copy-start(bf16[96,32]{0,1:T(8,128)(2,1)} %param.27) | copy-start | bytes 18436
  253.1 3.4 copy-start.6
  253.1 3.4 copy-start.9
  253.1 3.5 copy-start.8
  328.3 6.8 %copy-start.10 = (bf16[2,32,96]{2,1,0:T(8,128)(2,1)S(1)}, bf16[2,32,96]{2,1,0:T(8,128)(2,1)}, u32[]{:S(2)}) copy-start(bf16[2,32,96]{2,1,0:T(8,128)(2,1)} %param.28) | copy-start | bytes 36868
  335.1 1.7 copy-start.5
  338.4 1.4 copy-start.1
  345.5 9.5 %collective-permute-start.4 = (bf16[102,96,3]{0,1,2:T(8,128)(2,1)S(1)}, bf16[102,96,3]{0,1,2:T(8,128)(2,1)S(1)}, u32[]{:S(2)}, u32[]{:S(2)}) collective-permute-start(bf16[102,96,3]{0,1,2:T(8,128)(2,1)S(1)} %copy.40), channel_id=1, source_target_pairs={{0,1},{1,2},{2,3},{3,4},{4,5},{5,6},{6,7},{7,0},{8,9},{9,10},{10,1... | collective-permute-start | bytes 176264 | tf_op jit(solution)/shard_map/ppermute | solution.py:15
  349.2 8.8 %collective-permute-start.5 = (bf16[102,96,3]{0,1,2:T(8,128)(2,1)S(1)}, bf16[102,96,3]{0,1,2:T(8,128)(2,1)S(1)}, u32[]{:S(2)}, u32[]{:S(2)}) collective-permute-start(bf16[102,96,3]{0,1,2:T(8,128)(2,1)S(1)} %copy.42), channel_id=1, source_target_pairs={{1,0},{2,1},{3,2},{4,3},{5,4},{6,5},{7,6},{0,7},{9,8},{10,9},{11,1... | collective-permute-start | bytes 176264 | tf_op jit(solution)/shard_map/ppermute | solution.py:17
  444.8 3.7 copy-start.2
  444.8 3.7 copy-start.17
  444.9 3.7 copy-start.19
  444.9 3.7 copy-start.20
  448.5 12.7 %copy-start.11 = (bf16[8,96]{1,0:T(8,128)(2,1)S(1)}, bf16[8,96]{1,0:T(8,128)(2,1)}, u32[]{:S(2)}) copy-start(bf16[8,96]{1,0:T(8,128)(2,1)} %param.35) | copy-start | bytes 4612
  448.5 12.6 %copy-start.12 = (bf16[96,8]{0,1:T(8,128)(2,1)S(1)}, bf16[96,8]{0,1:T(8,128)(2,1)}, u32[]{:S(2)}) copy-start(bf16[96,8]{0,1:T(8,128)(2,1)} %param.34) | copy-start | bytes 4612
Sparse Core Ops, SparseCore 0:
  256.6 71.6 all-gather.2
